TPU v7x, 256 devices: a whole 4x4x8 slice. The times are simulated.
256 devices in a mesh: prow: 32 (over x, z), pcol: 8 (over y, core).
Axes of the slice: x: 4, y: 4, z: 8, core: 2. Of those that a mesh axis runs over, the one named last changes fastest.
Arguments:
- anc_inverse: bfloat16 [4, 32, 256, 16, 8, 256], P(None, 'prow', None, None, 'pcol'), may hold values from -6 to 6
- first_lower: bfloat16 [4, 32, 256, 256], P(None, 'prow', 'pcol'), may hold values from -0.046875 to 0.046875
- second_lower: bfloat16 [4, 32, 256, 256], P(None, 'prow', 'pcol'), may hold values from -0.0546875 to 0.0546875
- second_top: bfloat16 [256, 256], replicated, may hold values from -0.3125 to 0.3125
- struct_first: int32 [128], replicated, may hold values from 0 to 1
- struct_keep: int32 [128], replicated, may hold values from 0 to 1
- pivot_h: float32 [2, 256, 256], replicated, as said below
- pivot_s: float32 [2, 256, 256], replicated, as said below
- shifts: float32 [40], replicated, may hold values from 0.5 to 4
- pole_index: int32 [40], replicated, may hold values from 0 to 39, each once
Outputs:
- first_column: bfloat16 [4, 32, 256, 256], P(None, 'prow', 'pcol')
- first_diag: float32 [256, 256], replicated
- link_column: bfloat16 [256, 256], replicated
- second_column: bfloat16 [4, 32, 256, 256], P(None, 'prow', 'pcol')
- second_diag: float32 [256, 256], replicated
Inputs may be any that keep to these rules, and one draw needn't show every extreme that they name: `struct_first`: 1 marks a block row of the first supernode's structure. `struct_keep`: 1 marks a structure block that the second supernode keeps. `pole_index`: each pole appears once. `pivot_h`: symmetric, with a positive diagonal larger than each row's off-diagonal magnitudes together. `pivot_s`: symmetric, with a positive diagonal larger than each row's off-diagonal magnitudes together.
All inputs are finite; a program needn't handle non-finite values.
Results may differ from a plain program's by a relative error of at most 0.0041.
The roundings to bfloat16 on the way count: a program that leaves them out, or rounds other values in their place, can miss the bound.
Values may be sent and summed in bfloat16 or wider, within the bound.
A program may use at most 64 MiB of HBM per device.

v0:
```python
import jax
import jax.numpy as jnp
from jax import lax
from jax.sharding import PartitionSpec as P


def pivot_inverse(h_block, s_block, shift):
    factor = jnp.linalg.cholesky(h_block + shift * s_block)
    identity = jnp.eye(h_block.shape[0], dtype=jnp.float32)
    return jax.scipy.linalg.cho_solve((factor, True), identity)


def local_mask(flags, row_blocks, grid_rows, my_row):
    table = flags.reshape(row_blocks, grid_rows).astype(jnp.float32)
    return lax.dynamic_index_in_dim(table, my_row, axis=1, keepdims=False)


def per_device(
    anc_inverse,
    first_lower,
    second_lower,
    second_top,
    struct_first,
    struct_keep,
    pivot_h,
    pivot_s,
    shifts,
    pole_index,
):
    grid_rows = lax.axis_size("prow")
    grid_cols = lax.axis_size("pcol")
    my_row = lax.axis_index("prow")
    my_col = lax.axis_index("pcol")
    row_blocks = first_lower.shape[0]
    slab = first_lower.shape[2]
    width = first_lower.shape[3]
    col_blocks = anc_inverse.shape[3]
    first_mask = local_mask(struct_first, row_blocks, grid_rows, my_row)
    second_mask = first_mask * local_mask(struct_keep, row_blocks, grid_rows, my_row)
    lower_first = first_lower[:, 0] * first_mask.astype(jnp.bfloat16)[:, None, None]
    lower_second = second_lower[:, 0] * second_mask.astype(jnp.bfloat16)[:, None, None]
    stacked = jnp.concatenate([lower_first, lower_second], axis=2)[:, None]
    gathered = lax.all_gather(stacked, "prow", axis=1, tiled=True)
    grouped = gathered.reshape(row_blocks, grid_rows // grid_cols, grid_cols, slab, 2 * width)
    columns = lax.all_to_all(grouped, "pcol", split_axis=2, concat_axis=3, tiled=True)
    column_blocks = columns.reshape(col_blocks, width, 2 * width)
    inverse_rows = anc_inverse.reshape(row_blocks, width, col_blocks, width)
    totals = lax.psum(
        jnp.einsum(
            "axcy,cyz->xaz", inverse_rows, column_blocks, preferred_element_type=jnp.float32
        ),
        "pcol",
    )
    row_part = lax.dynamic_slice_in_dim(totals, my_col * slab, slab, 0)
    first_col = (-row_part[:, :, :width] * first_mask[None, :, None]).astype(jnp.bfloat16)
    bridge = jnp.einsum("raw,wz->raz", first_col, second_top, preferred_element_type=jnp.float32)
    second_col = (-(row_part[:, :, width:] + bridge) * second_mask[None, :, None]).astype(
        jnp.bfloat16
    )
    first_rows = lower_first.transpose(1, 0, 2)
    second_rows = lower_second.transpose(1, 0, 2)
    first_term = jnp.einsum(
        "ray,raz->yz", first_rows, first_col, preferred_element_type=jnp.float32
    )
    cross_term = jnp.einsum(
        "ray,raz->yz", first_col, second_rows, preferred_element_type=jnp.float32
    )
    second_term = jnp.einsum(
        "ray,raz->yz", second_rows, second_col, preferred_element_type=jnp.float32
    )
    first_sum, cross_sum, second_sum = lax.psum(
        (first_term, cross_term, second_term), ("prow", "pcol")
    )
    poles = jnp.arange(shifts.shape[0], dtype=jnp.int32)
    shift = jnp.sum(jnp.where(poles == pole_index[0], shifts, 0.0))
    first_diag = pivot_inverse(pivot_h[0], pivot_s[0], shift) - first_sum
    link_col = (
        -(
            cross_sum
            + jnp.dot(
                first_diag.astype(jnp.bfloat16), second_top, preferred_element_type=jnp.float32
            )
        )
    ).astype(jnp.bfloat16)
    second_diag = (
        pivot_inverse(pivot_h[1], pivot_s[1], shift)
        - second_sum
        - jnp.einsum("yz,yw->zw", second_top, link_col, preferred_element_type=jnp.float32)
    )
    return (
        first_col.transpose(1, 0, 2)[:, None],
        first_diag,
        link_col,
        second_col.transpose(1, 0, 2)[:, None],
        second_diag,
    )


def solution(mesh):
    return jax.shard_map(
        per_device,
        mesh=mesh,
        in_specs=(
            P(None, "prow", None, None, "pcol", None),
            P(None, "prow", "pcol", None),
            P(None, "prow", "pcol", None),
            P(),
            P(),
            P(),
            P(),
            P(),
            P(),
            P(),
        ),
        out_specs=(P(None, "prow", "pcol", None), P(), P(), P(None, "prow", "pcol", None), P()),
        check_vma=False,
    )
```

profile of v0, /device:TPU:8, one launch (start us, length us, event | category | flops | bytes accessed | tf_op | source)
XLA Modules:
  0.0 544.1 jit_solution(14048645056738182097)
XLA Ops:
  7.2 0.7 convert_element_type.47
  8.0 0.7 convert_element_type.44
  9.0 0.9 bitcast_multiply_fusion
  9.9 0.9 bitcast_multiply_fusion.1
  10.8 0.7 pad_maximum_fusion
  11.5 1.1 fusion.48
  12.7 1.1 fusion.47
  13.9 1.9 fusion.43
  15.8 0.7 fusion.23
  16.9 0.7 fusion.22
  17.7 0.7 fusion.11
  18.5 11.7 %cholesky.130 = f32[128,128]{1,0:T(8,128)S(1)} custom-call(f32[128,128]{1,0:T(8,128)S(1)} %cholesky.194), custom_call_target="Cholesky" | custom-call | tf_op jit(solution)/shard_map/jit(cholesky)/cholesky | solution.py:8
  30.3 9.8 %custom-call.15 = f32[1,128,128]{1,2,0:T(8,128)S(1)} custom-call(f32[1,128,128]{2,1,0:T(8,128)S(1)} %get-tuple-element.84), custom_call_target="InvertDiagBlocksLowerTriangular" | custom-call | tf_op jit(solution)/shard_map/jit(cholesky)/cholesky | solution.py:8
  40.6 11.7 %cholesky.147 = f32[128,128]{1,0:T(8,128)S(1)} custom-call(f32[128,128]{1,0:T(8,128)S(1)} %convolution_subtract_fusion.5), custom_call_target="Cholesky" | custom-call | tf_op jit(solution)/shard_map/jit(cholesky)/cholesky | solution.py:8
  52.3 0.6 compare_reduce_fusion.3
  53.0 0.6 compare_reduce_fusion.2
  55.0 41.5 %all-gather.3.cloned.1.call-done = bf16[4,1024,512]{2,1,0:T(8,128)(2,1)} async-done(((bf16[4,32,512]{2,1,0:T(8,128)(2,1)}), bf16[4,1024,512]{2,1,0:T(8,128)(2,1)}) %all-gather.3.cloned.1.call-update) | async-done | bytes 4194320 | tf_op jit(solution)/shard_map/all_gather | solution.py:43
  96.5 4.7 copy.82
  101.2 5.2 all-to-all-start
  106.4 4.0 while.4
  106.5 0.6 fusion.74
  107.0 1.4 bitcast_dynamic-update-slice_fusion.4
  108.5 0.6 fusion.74
  109.0 1.4 bitcast_dynamic-update-slice_fusion.4
  110.4 19.7 %custom-call.16 = f32[2,128,128]{1,2,0:T(8,128)S(1)} custom-call(f32[2,128,128]{2,1,0:T(8,128)S(1)} %get-tuple-element.21), custom_call_target="InvertDiagBlocksLowerTriangular" | custom-call | tf_op jit(solution)/shard_map/jit(_cho_solve)/triangular_solve | solution.py:10
  130.1 11.7 %cholesky.164 = f32[128,128]{1,0:T(8,128)S(1)} custom-call(f32[128,128]{1,0:T(8,128)S(1)} %cholesky.197), custom_call_target="Cholesky" | custom-call | tf_op jit(solution)/shard_map/jit(cholesky)/cholesky | solution.py:8
  141.9 9.8 %custom-call.17 = f32[1,128,128]{1,2,0:T(8,128)S(1)} custom-call(f32[1,128,128]{2,1,0:T(8,128)S(1)} %get-tuple-element.80), custom_call_target="InvertDiagBlocksLowerTriangular" | custom-call | tf_op jit(solution)/shard_map/jit(cholesky)/cholesky | solution.py:8
  152.2 11.7 %cholesky.181 = f32[128,128]{1,0:T(8,128)S(1)} custom-call(f32[128,128]{1,0:T(8,128)S(1)} %convolution_subtract_fusion.4), custom_call_target="Cholesky" | custom-call | tf_op jit(solution)/shard_map/jit(cholesky)/cholesky | solution.py:8
  163.9 0.6 compare_reduce_fusion.1
  164.6 0.6 compare_reduce_fusion
  166.6 4.0 while.5
  167.2 1.4 bitcast_dynamic-update-slice_fusion.5
  168.6 0.6 fusion.75
  169.2 1.4 bitcast_dynamic-update-slice_fusion.5
  170.6 19.9 %custom-call.18 = f32[2,128,128]{1,2,0:T(8,128)S(1)} custom-call(f32[2,128,128]{2,1,0:T(8,128)S(1)} %get-tuple-element.22), custom_call_target="InvertDiagBlocksLowerTriangular" | custom-call | tf_op jit(solution)/shard_map/jit(_cho_solve)/triangular_solve | solution.py:10
  192.3 2.5 copy.83
  194.8 9.6 %fusion.2 = f32[256,4,512]{2,0,1:T(8,128)} fusion(bf16[16,256,512,1]{2,1,0,3:T(8,128)(2,1)S(1)} %bitcast.134, bf16[4,256,16,256]{3,2,1,0:T(8,128)(2,1)} %bitcast.136), kind=kOutput, calls=%fused_computation.6 | convolution fusion | flops 4294967296 | bytes 14680064 | tf_op jit(solution)/shard_map/axcy,cyz->xaz/dot_general | solution.py:49
  206.0 64.4 %all-reduce.5.cloned.1.call-done = f32[256,4,512]{2,0,1:T(8,128)} async-done(((f32[256,4,512]{2,0,1:T(8,128)}), f32[256,4,512]{2,0,1:T(8,128)}) %all-reduce.5.cloned.1.call-update) | async-done | bytes 2097168 | tf_op jit(solution)/shard_map/psum | solution.py:48
  270.3 1.0 fusion.15
  271.3 0.9 convolution_bitcast_fusion.3
  272.2 0.9 convolution_bitcast_fusion.2
  273.1 1.1 fusion.10
  274.2 0.9 convolution_bitcast_fusion.1
  275.5 1.6 fusion.71
  277.1 256.3 %all-reduce.7.cloned.1.call-done = (f32[256,256]{1,0:T(8,128)}, f32[256,256]{1,0:T(8,128)}, f32[256,256]{1,0:T(8,128)}) async-done(((f32[256,256]{1,0:T(8,128)}, f32[256,256]{1,0:T(8,128)}, f32[256,256]{1,0:T(8,128)}), (f32[256,256]{1,0:T(8,128)}, f32[256,256]{1,0:T(8,128)}, f32[256,256]{1,0:T(8,128)})) %all-reduce.7.cloned.1.call-update) | async-done | bytes 786448 | tf_op jit(solution)/shard_map/psum | solution.py:71
  533.4 1.0 maximum_subtract_fusion
  534.4 1.2 fusion.7
  535.6 1.9 fusion.6
  (61 shorter events, 6.7 us)
Async XLA Ops:
  7.2 266.0 %copy-start = (bf16[256,256]{1,0:T(8,128)(2,1)S(1)}, bf16[256,256]{1,0:T(8,128)(2,1)}, u32[]{:S(2)}) copy-start(bf16[256,256]{1,0:T(8,128)(2,1)} %param.16) | copy-start | bytes 393220
  7.2 89.3 %all-gather.3.cloned.1.call-start = ((), (), s32[]{:S(2)}) async-start(), calls=%async_computation.2 | async-start | bytes 4325376 | tf_op jit(solution)/shard_map/all_gather | solution.py:43
  101.2 91.1 %all-to-all-start = ((bf16[4,4,8,32,512]{4,3,1,0,2:T(8,128)(2,1)}), bf16[4,4,8,32,512]{4,3,1,0,2:T(8,128)(2,1)}, u32[]{:S(2)}, u32[]{:S(2)}) async-start(bf16[4,4,8,32,512]{4,3,1,0,2:T(8,128)(2,1)} %copy.82), calls=%async_computation | async-start | bytes 8388608 | tf_op jit(solution)/shard_map/all_to_all | solution.py:45
  106.4 164.0 %all-reduce.5.cloned.1.call-start = ((), (), s32[]{:S(2)}) async-start(), calls=%async_computation.1 | async-start | bytes 4194304 | tf_op jit(solution)/shard_map/psum | solution.py:48
  204.4 329.0 %all-reduce.7.cloned.1.call-start = ((), (), s32[]{:S(2)}) async-start(), calls=%async_computation.3 | async-start | bytes 1572864 | tf_op jit(solution)/shard_map/psum | solution.py:71
  274.2 263.3 %copy-start.3 = (bf16[32,4,256]{2,0,1:T(8,128)(2,1)}, bf16[32,4,256]{2,0,1:T(8,128)(2,1)S(1)}, u32[]{:S(2)}) copy-start(bf16[32,4,256]{2,0,1:T(8,128)(2,1)S(1)} %fusion.10) | copy-start | bytes 196612
  534.4 3.2 copy-start.1
  535.6 2.0 copy-start.2
Sparse Core Ops, SparseCore 0:
  11.6 84.8 all-gather.2
  204.5 65.7 all-reduce.4
  276.7 256.6 all-reduce.6
where the time goes:
time: 545 us; the launch traced here: 544 us
  waiting for transfers between devices  362 us (66%)
  other arithmetic  120 us (22%)
  matrix products  20.9 us (4%)
  local copies, waits for them, and re-layouts  18.6 us (3%)
  between operations  16.7 us (3%)
    psum x1, waiting for transfers between devices, per_device(): lax.psum((first_term, cross_term, second_term), ('prow', 'pcol'))  256 us
    another operation x14, other arithmetic, pivot_inverse(): factor = jnp.linalg.cholesky(h_block + shift * s_block)  69.2 us
    psum x1, waiting for transfers between devices, per_device(): lax.psum(jnp.einsum('axcy,cyz->xaz', inverse_rows, column_blocks, preferr...  64.4 us
    all_gather x1, waiting for transfers between devices, per_device(): gathered = lax.all_gather(stacked, 'prow', axis=1, tiled=True)  41.5 us
    another operation x5, other arithmetic, pivot_inverse(): return jax.scipy.linalg.cho_solve((factor, True), identity)  39.6 us
  transfers between devices with their start and end apart: 4, of which 3 were waited for; matrix products, arithmetic and copies ran while one was open for 24% of the time, Pallas kernels for 0%

commit v1 on v0

--- a/solution.py
+++ b/solution.py
@@ -2,6 +2,8 @@
 import jax.numpy as jnp
 from jax import lax
 from jax.sharding import PartitionSpec as P
+
+panel_render = lambda mat: jnp.sum(lax.all_gather(mat, axis_name="pcol"), axis=0)
 
 
 def pivot_inverse(h_block, s_block, shift):
@@ -45,11 +47,8 @@
     columns = lax.all_to_all(grouped, "pcol", split_axis=2, concat_axis=3, tiled=True)
     column_blocks = columns.reshape(col_blocks, width, 2 * width)
     inverse_rows = anc_inverse.reshape(row_blocks, width, col_blocks, width)
-    totals = lax.psum(
-        jnp.einsum(
-            "axcy,cyz->xaz", inverse_rows, column_blocks, preferred_element_type=jnp.float32
-        ),
-        "pcol",
+    totals = panel_render(
+        jnp.einsum("axcy,cyz->xaz", inverse_rows, column_blocks, preferred_element_type=jnp.float32)
     )
     row_part = lax.dynamic_slice_in_dim(totals, my_col * slab, slab, 0)
     first_col = (-row_part[:, :, :width] * first_mask[None, :, None]).astype(jnp.bfloat16)

time: 545 us -> 591 us (1.084)
  blocking collectives: 0 us -> 53.8 us
  waiting for transfers between devices: 362 us -> 334 us
  local copies, waits for them, and re-layouts: 18.6 us -> 30.6 us
  other arithmetic: 120 us -> 127 us
    psum x1 -> x0, waiting for transfers between devices: 64.4 us -> none  [per_device(): lax.psum(jnp.einsum('axcy,cyz->xaz', inverse_rows, column_blocks, preferr...]
    all_to_all x0 -> x1, blocking collectives: none -> 53.8 us  [per_device(): lax.all_to_all(grouped, 'pcol', split_axis=2, concat_axis=3, tiled=True)]
    all_gather x1, waiting for transfers between devices: 41.5 us -> 84.7 us  [per_device(): gathered = lax.all_gather(stacked, 'prow', axis=1, tiled=True)]
    unnamed x12 -> x33, local copies, waits for them, and re-layouts: 0.54 us -> 18.2 us
    reduce_sum x0 -> x1, other arithmetic: none -> 8.14 us  [jnp.sum(lax.all_gather(mat, axis_name='pcol'), axis=0)]
    psum x1, waiting for transfers between devices: 256 us -> 249 us  [per_device(): lax.psum((first_term, cross_term, second_term), ('prow', 'pcol'))]
  transfers between devices with their start and end apart: 4 -> 3, of which waited for: 3 -> 2; matrix products, arithmetic and copies ran while one was open for 24% -> 22% of each run, Pallas kernels for 0% -> 0%
where the time goes in v1:
time: 591 us; the launch traced here: 586 us
  waiting for transfers between devices  334 us (57%)
  other arithmetic  127 us (21%)
  blocking collectives  53.8 us (9%)
  local copies, waits for them, and re-layouts  30.6 us (5%)
  matrix products  22.5 us (4%)
  between operations  17.1 us (3%)
    psum x1, waiting for transfers between devices, per_device(): lax.psum((first_term, cross_term, second_term), ('prow', 'pcol'))  249 us
    all_gather x1, waiting for transfers between devices, per_device(): gathered = lax.all_gather(stacked, 'prow', axis=1, tiled=True)  84.7 us
    another operation x14, other arithmetic, pivot_inverse(): factor = jnp.linalg.cholesky(h_block + shift * s_block)  69.2 us
    all_to_all x1, blocking collectives, per_device(): lax.all_to_all(grouped, 'pcol', split_axis=2, concat_axis=3, tiled=True)  53.8 us
    another operation x5, other arithmetic, pivot_inverse(): return jax.scipy.linalg.cho_solve((factor, True), identity)  39.6 us
    unnamed x33, local copies, waits for them, and re-layouts  18.2 us
  transfers between devices with their start and end apart: 3, of which 2 were waited for; matrix products, arithmetic and copies ran while one was open for 22% of the time, Pallas kernels for 0%

profile of v1, /device:TPU:8, one launch (start us, length us, event | category | flops | bytes accessed | tf_op | source)
XLA Modules:
  0.0 585.5 jit_solution(2530771170444857881)
XLA Ops:
  7.2 0.7 convert_element_type.47
  8.0 0.7 convert_element_type.44
  9.0 0.9 bitcast_multiply_fusion
  9.9 1.6 bitcast_multiply_fusion.1
  11.5 1.5 pad_maximum_fusion
  13.0 84.7 %all-gather.5.cloned.1.call-done = bf16[4,1024,512]{2,1,0:T(8,128)(2,1)} async-done(((bf16[4,32,512]{2,1,0:T(8,128)(2,1)}), bf16[4,1024,512]{2,1,0:T(8,128)(2,1)}) %all-gather.5.cloned.1.call-update) | async-done | bytes 4194320 | tf_op jit(solution)/shard_map/all_gather | solution.py:45
  97.8 2.7 copy.50
  100.5 53.8 %all_to_all.4 = bf16[4,4,8,32,512]{4,3,1,0,2:T(8,128)(2,1)S(1)} all-to-all(bf16[4,4,8,32,512]{4,3,1,0,2:T(8,128)(2,1)S(1)} %copy.50), channel_id=1, replica_groups=mesh['prow'=32,'pcol'=8] {'pcol'}, dimensions={2} | all-to-all | bytes 8388608 | tf_op jit(solution)/shard_map/all_to_all | solution.py:47
  154.8 1.6 slice-done.1
  156.4 7.2 %fusion.2 = f32[256,4,512]{0,2,1:T(8,128)} fusion(bf16[16,256,512,1]{2,1,0,3:T(8,128)(2,1)S(1)} %bitcast.143, bf16[4,256,16,256]{3,2,1,0:T(8,128)(2,1)S(1)} %bitcast.147), kind=kOutput, calls=%fused_computation.6 | convolution fusion | flops 4294967296 | bytes 14680064 | tf_op jit(solution)/shard_map/axcy,cyz->xaz/dot_general | solution.py:51
  164.6 0.6 fusion.41
  165.2 0.7 fusion.21
  166.3 0.7 fusion.20
  167.1 0.7 fusion.11
  167.9 11.7 %cholesky.130 = f32[128,128]{1,0:T(8,128)S(1)} custom-call(f32[128,128]{1,0:T(8,128)S(1)} %cholesky.194), custom_call_target="Cholesky" | custom-call | tf_op jit(solution)/shard_map/jit(cholesky)/cholesky | solution.py:10
  179.7 9.8 %custom-call.15 = f32[1,128,128]{1,2,0:T(8,128)S(1)} custom-call(f32[1,128,128]{2,1,0:T(8,128)S(1)} %get-tuple-element.81), custom_call_target="InvertDiagBlocksLowerTriangular" | custom-call | tf_op jit(solution)/shard_map/jit(cholesky)/cholesky | solution.py:10
  190.0 11.7 %cholesky.147 = f32[128,128]{1,0:T(8,128)S(1)} custom-call(f32[128,128]{1,0:T(8,128)S(1)} %convolution_subtract_fusion.5), custom_call_target="Cholesky" | custom-call | tf_op jit(solution)/shard_map/jit(cholesky)/cholesky | solution.py:10
  201.7 0.6 compare_reduce_fusion.3
  202.4 0.6 compare_reduce_fusion.2
  204.4 4.2 while.4
  204.6 0.6 fusion.72
  205.2 1.4 bitcast_dynamic-update-slice_fusion.4
  206.6 0.6 fusion.72
  207.2 1.4 bitcast_dynamic-update-slice_fusion.4
  208.6 19.7 %custom-call.16 = f32[2,128,128]{1,2,0:T(8,128)S(1)} custom-call(f32[2,128,128]{2,1,0:T(8,128)S(1)} %get-tuple-element.21), custom_call_target="InvertDiagBlocksLowerTriangular" | custom-call | tf_op jit(solution)/shard_map/jit(_cho_solve)/triangular_solve | solution.py:12
  228.3 11.7 %cholesky.164 = f32[128,128]{1,0:T(8,128)S(1)} custom-call(f32[128,128]{1,0:T(8,128)S(1)} %cholesky.197), custom_call_target="Cholesky" | custom-call | tf_op jit(solution)/shard_map/jit(cholesky)/cholesky | solution.py:10
  240.1 9.8 %custom-call.17 = f32[1,128,128]{1,2,0:T(8,128)S(1)} custom-call(f32[1,128,128]{2,1,0:T(8,128)S(1)} %get-tuple-element.77), custom_call_target="InvertDiagBlocksLowerTriangular" | custom-call | tf_op jit(solution)/shard_map/jit(cholesky)/cholesky | solution.py:10
  250.4 11.7 %cholesky.181 = f32[128,128]{1,0:T(8,128)S(1)} custom-call(f32[128,128]{1,0:T(8,128)S(1)} %convolution_subtract_fusion.4), custom_call_target="Cholesky" | custom-call | tf_op jit(solution)/shard_map/jit(cholesky)/cholesky | solution.py:10
  262.1 0.6 compare_reduce_fusion.1
  262.8 0.6 compare_reduce_fusion
  264.8 4.0 while.5
  264.8 0.6 fusion.73
  265.4 1.4 bitcast_dynamic-update-slice_fusion.5
  267.4 1.4 bitcast_dynamic-update-slice_fusion.5
  268.8 19.9 %custom-call.18 = f32[2,128,128]{1,2,0:T(8,128)S(1)} custom-call(f32[2,128,128]{2,1,0:T(8,128)S(1)} %get-tuple-element.22), custom_call_target="InvertDiagBlocksLowerTriangular" | custom-call | tf_op jit(solution)/shard_map/jit(_cho_solve)/triangular_solve | solution.py:12
  290.2 0.9 fusion.31
  292.3 1.0 convolution_subtract_fusion
  293.3 15.7 %copy.75 = f32[256,8,8,256]{3,2,1,0:T(8,128)} copy(f32[256,8,8,256]{3,1,2,0:T(8,128)} %bitcast.141) | data formatting | bytes 33554432
  309.0 8.1 %reduce_sum.18 = f32[256,4,512]{0,2,1:T(8,128)S(1)} reduce(f32[8,256,4,512]{1,0,3,2:T(8,128)} %bitcast.140, f32[]{:T(128)} %constant.84.clone.1), dimensions={0}, to_apply=%region_0.1 | reduce | flops 3670016 | bytes 18874372 | tf_op jit(solution)/shard_map/reduce_sum | solution.py:6
  317.7 1.8 convolution_bitcast_fusion.3
  319.5 1.8 convolution_bitcast_fusion.2
  321.6 1.8 convolution_bitcast_fusion.1
  323.4 1.2 fusion.34
  324.6 0.7 fusion.69
  325.3 249.2 %all-reduce.4.cloned.1.call-done = (f32[256,256]{1,0:T(8,128)}, f32[256,256]{1,0:T(8,128)}, f32[256,256]{1,0:T(8,128)}) async-done(((f32[256,256]{1,0:T(8,128)}, f32[256,256]{1,0:T(8,128)}, f32[256,256]{1,0:T(8,128)}), (f32[256,256]{1,0:T(8,128)}, f32[256,256]{1,0:T(8,128)}, f32[256,256]{1,0:T(8,128)})) %all-reduce.4.cloned.1.call-update) | async-done | bytes 786448 | tf_op jit(solution)/shard_map/psum | solution.py:70
  574.6 1.0 maximum_subtract_fusion
  575.5 1.2 fusion.7
  576.8 1.9 fusion.6
  (84 shorter events, 8.0 us)
Async XLA Ops:
  7.2 314.2 %copy-start = (bf16[256,256]{1,0:T(8,128)(2,1)S(1)}, bf16[256,256]{1,0:T(8,128)(2,1)}, u32[]{:S(2)}) copy-start(bf16[256,256]{1,0:T(8,128)(2,1)} %param.16) | copy-start | bytes 393220
  7.2 90.6 %all-gather.5.cloned.1.call-start = ((), (), s32[]{:S(2)}) async-start(), calls=%async_computation.1 | async-start | bytes 4325376 | tf_op jit(solution)/shard_map/all_gather | solution.py:45
  9.9 1.6 copy-start.2
  13.0 280.3 %all-gather.7.cloned.1.call-start = ((), (), s32[]{:S(2)}) async-start(), calls=%async_computation.2 | async-start | bytes 18874368 | tf_op jit(solution)/shard_map/all_gather | solution.py:6
  100.4 54.4 %slice-start = ((s8[8388608]{0:T(1024)(128)(4,1)}), s8[4194304]{0:T(1024)(128)(4,1)S(1)}, s32[]{:S(2)}) async-start(s8[8388608]{0:T(1024)(128)(4,1)} %bitcast.145), calls=%async_computation.4 | async-start | bytes 8388608
  154.2 2.2 slice-start.1
  156.4 7.8 %copy-start.4 = (f32[2,256,256]{2,1,0:T(8,128)S(1)}, f32[2,256,256]{2,1,0:T(8,128)}, u32[]{:S(2)}) copy-start(f32[2,256,256]{2,1,0:T(8,128)} %param.19) | copy-start | bytes 1572868
  156.4 8.0 %copy-start.5 = (f32[2,256,256]{2,1,0:T(8,128)S(1)}, f32[2,256,256]{2,1,0:T(8,128)}, u32[]{:S(2)}) copy-start(f32[2,256,256]{2,1,0:T(8,128)} %param.20) | copy-start | bytes 1572868
  163.6 0.9 copy-start.9
  163.6 0.9 copy-start.10
  163.7 410.9 %all-reduce.4.cloned.1.call-start = ((), (), s32[]{:S(2)}) async-start(), calls=%async_computation.3 | async-start | bytes 1572864 | tf_op jit(solution)/shard_map/psum | solution.py:70
  288.7 20.3 %copy-start.3 = (f32[2,128,128]{1,2,0:T(8,128)}, f32[2,128,128]{1,2,0:T(8,128)S(1)}, u32[]{:S(2)}) copy-start(f32[2,128,128]{1,2,0:T(8,128)S(1)} %custom-call.18) | copy-start | bytes 393220
  317.5 257.1 %copy-start.6 = (f32[128,256]{1,0:T(8,128)S(1)}, f32[128,256]{1,0:T(8,128)}, u32[]{:S(2)}) copy-start(f32[128,256]{1,0:T(8,128)} %fusion.31) | copy-start | bytes 393220
  321.6 257.1 %copy-start.8 = (bf16[32,4,256]{2,0,1:T(8,128)(2,1)}, bf16[32,4,256]{2,0,1:T(8,128)(2,1)S(1)}, u32[]{:S(2)}) copy-start(bf16[32,4,256]{2,0,1:T(8,128)(2,1)S(1)} %fusion.10) | copy-start | bytes 196612
  575.5 3.2 copy-start.1
  576.8 2.0 copy-start.7
Sparse Core Ops, SparseCore 0:
  13.1 84.6 all-gather.4
  163.8 83.5 all-gather.6
  323.5 250.9 all-reduce.3
